TPU v7x, 32 devices: a whole 2x2x4 slice. The times are simulated.
32 devices in a mesh: outer: 2 (over x), inner: 4 (over y, core), cell: 4 (over z).
Axes of the slice: x: 2, y: 2, z: 4, core: 2. Of those that a mesh axis runs over, the one named last changes fastest.
Arguments:
- premium: float32 [48, 8192], P('outer', 'cell'), may hold values from 0.1 to 1
- charge: float32 [48, 8192], P('outer', 'cell'), may hold values from 0.05 to 2
- mortality: float32 [48, 8192], P('outer', 'cell'), may hold values from 0.0005 to 0.01
- lapse_table: float32 [16, 48], replicated, may hold values from 0.001 to 0.02
- lapse_index: int32 [8192], P('cell'), may hold values from 0 to 15
- guarantee_type: int32 [8192], P('cell'), may hold values from 0 to 2
- block_index: int32 [8192], P('cell'), may hold values from 0 to 255, never falling along the last dimension, each value on 1 to 128 neighbouring positions
- account_start: float32 [8192], P('cell'), may hold values from 5 to 50
- guarantee_start: float32 [8192], P('cell'), may hold values from 5 to 60
- fee_rate: float32 [8192], P('cell'), may hold values from 0.0003 to 0.002
- first_rates: float32 [8, 64, 36], P('outer', 'inner'), may hold values from 0 to 0.006
- second_rates: float32 [8, 64, 24], P('outer', 'inner'), may hold values from 0 to 0.006
- world_rates: float32 [8, 24], P('outer'), may hold values from 0 to 0.006
- spread: float32 [8], P('outer'), may hold values from 0.0005 to 0.002
Outputs:
- cell_reserve: float32 [2, 8, 8192], P(None, ('outer', 'inner'), 'cell')
- block_reserve: float32 [2, 8, 256], P(None, ('outer', 'inner'), 'cell')
- capital: float32 [1], replicated
Inputs may be any that keep to these rules, and one draw needn't show every extreme that they name: `block_index`: block numbers never fall along the cells; every block holds 1 to 128 cells.
All inputs are finite; a program needn't handle non-finite values.
Results may differ from a plain program's by a relative error of at most 0.0003.
Values sent between devices are 32-bit elements; how exact they have to be, the bound alone decides.
A program may use at most 64 MiB of HBM per device.

v0:
```python
import functools
import jax
import jax.numpy as jnp
from jax import lax
from jax.experimental import pallas as pl
from jax.experimental.pallas import tpu as pltpu
from jax.sharding import PartitionSpec as P

PERIOD = 12
BLOCK = 128
LANES = 128
ROWS = 8

credit_floor = 0.001
rollup_growth = 0.05
VMEM = pl.BlockSpec(memory_space=pltpu.VMEM)


def tiles(x, count):
    return jnp.concatenate([x] * count, axis=1)


def month(account, surviving, growth, nf, om, lb, keep, inverse):
    credited = jnp.maximum(account * keep + nf, 0.0) * growth
    lapse = lb * jnp.clip(credited * inverse, 0.5, 1.5)
    return credited, surviving * (om - lapse)


def claims_of(account, credited, surviving, guarantee, mf):
    return surviving * (mf * jnp.maximum(guarantee - credited, 0.0) - account)


def anniversary(account, guarantee, ratchet, rollup):
    return (
        guarantee
        + ratchet * (jnp.maximum(guarantee, account) - guarantee)
        + rollup * rollup_growth * guarantee
    )


def prefix(rates):
    months = rates.shape[1]
    tri = (
        lax.broadcasted_iota(jnp.int32, (months, months), 0)
        <= lax.broadcasted_iota(jnp.int32, (months, months), 1)
    ).astype(jnp.float32)
    return jnp.dot(rates, tri, precision=lax.Precision.HIGHEST, preferred_element_type=jnp.float32)


def spread_lanes(values, target, rows):
    for m in range(values.shape[1]):
        target[m, rows, :] = jnp.broadcast_to(values[:, m : m + 1], (values.shape[0], LANES))


def year(start, plans, cell, growth_lanes, first_month, state, width):
    nf_ref, mf_ref, om_ref, lb_ref = plans
    total = nf_ref.shape[1]
    repeat = width // LANES

    def chunk(j, _):
        cols = pl.ds(pl.multiple_of(j * width, width), width)
        account, surviving, guarantee = start(cols)
        keep, ratchet, rollup = cell[0:1, cols], cell[1:2, cols], cell[2:3, cols]
        inverse = 1.0 / guarantee
        for m in range(PERIOD):
            row = slice(first_month + m, first_month + m + 1)
            account, surviving = month(
                account,
                surviving,
                tiles(growth_lanes[m], repeat),
                nf_ref[row, cols],
                om_ref[row, cols],
                lb_ref[row, cols],
                keep,
                inverse,
            )
        state[0, :, cols] = account
        state[1, :, cols] = surviving
        state[2, :, cols] = anniversary(account, guarantee, ratchet, rollup)
        return 0

    lax.fori_loop(0, total // width, chunk, 0)


def inner(state, plans, cell, gb, db, first_month, low, high, paths, sums, width):
    nf_ref, mf_ref, om_ref, lb_ref = plans
    total = nf_ref.shape[1]
    repeat = width // LANES
    months = db.shape[0]
    groups = paths // ROWS
    chunks = total // width

    def block(step, _):
        o, j = low + step // chunks, step % chunks
        cols = pl.ds(pl.multiple_of(j * width, width), width)
        keep, ratchet, rollup = cell[0:1, cols], cell[1:2, cols], cell[2:3, cols]
        shape = (ROWS, width)
        one = pl.ds(o, 1)
        account = [jnp.broadcast_to(state[0, one, cols], shape)] * groups
        surviving = [jnp.broadcast_to(state[1, one, cols], shape)] * groups
        guarantee = [jnp.broadcast_to(state[2, one, cols], shape)] * groups
        inverse = [1.0 / guarantee[0]] * groups
        rows = [pl.ds(pl.multiple_of(o * paths + g * ROWS, ROWS), ROWS) for g in range(groups)]
        present = jnp.zeros(shape, jnp.float32)
        for m in range(months):
            row = slice(first_month + m, first_month + m + 1)
            nf, mf, om, lb = nf_ref[row, cols], mf_ref[row, cols], om_ref[row, cols], lb_ref[row, cols]
            for g in range(groups):
                before, alive = account[g], surviving[g]
                account[g], surviving[g] = month(
                    before, alive, tiles(gb[m, rows[g], :], repeat), nf, om, lb, keep, inverse[g]
                )
                claims = claims_of(before, account[g], alive, guarantee[g], mf)
                present = present + tiles(db[m, rows[g], :], repeat) * claims
            if (m + 1) % PERIOD == 0 and m + 1 < months:
                for g in range(groups):
                    guarantee[g] = anniversary(account[g], guarantee[g], ratchet, rollup)
                    inverse[g] = 1.0 / guarantee[g]
        sums[o, :, cols] = present
        return 0

    lax.fori_loop(0, (high - low) * chunks, block, 0)


def reduce_rows(sums, out, low, high, scale):
    for o in range(low, high):
        out[o] = jnp.sum(sums[o], axis=0, keepdims=True) * scale


def fill_growth(rates_ref, spread_column, gb, low, high, paths):
    for o in range(low, high):
        for g in range(paths // ROWS):
            rows = slice(o * paths + g * ROWS, o * paths + (g + 1) * ROWS)
            spread_lanes(
                1.0 + jnp.maximum(rates_ref[rows, :] - spread_column[o : o + 1], credit_floor), gb, rows
            )


def fill_discount(rates_ref, db):
    discount = jnp.exp(-prefix(rates_ref[...]))
    for at in range(0, discount.shape[0], ROWS):
        spread_lanes(discount[at : at + ROWS], db, slice(at, at + ROWS))


def peers(axes):
    sizes = [lax.axis_size(axis) for axis in axes]
    count = 1
    place = 0
    for axis, size in zip(axes, sizes):
        place = place * size + lax.axis_index(axis)
        count *= size
    others = []
    for distance in range(1, count):
        index = lax.rem(place + distance, count)
        rest, device = index, {}
        for axis, size in reversed(list(zip(axes, sizes))):
            device[axis] = lax.rem(rest, size)
            rest = lax.div(rest, size)
        others.append((index, device))
    return place, others


def greet(groups):
    barrier = pltpu.get_barrier_semaphore()
    count = 0
    for others in groups:
        for _, device in others:
            pl.semaphore_signal(barrier, inc=1, device_id=device, device_id_type=pl.DeviceIdType.MESH)
            count += 1
    return barrier, count


def send(source, target, device, sems, at):
    copy = pltpu.make_async_remote_copy(
        src_ref=source,
        dst_ref=target,
        send_sem=sems.at[0, at],
        recv_sem=sems.at[1, at],
        device_id=device,
        device_id_type=pl.DeviceIdType.MESH,
    )
    copy.start()
    return copy


def finish(copies):
    for copy in copies:
        copy.wait()


def local_totals(partial, low, high):
    zero = jnp.zeros((1, LANES), jnp.float32)
    rows = [
        jnp.broadcast_to(jnp.sum(partial[o], axis=1, keepdims=True), (1, LANES)) if low <= o < high else zero
        for o in range(ROWS)
    ]
    return jnp.concatenate(rows, axis=0)


def whole_kernel(
    outers, paths, paths_all, cells_all, width,
    premium, charge, mortality, table_in, lapse_in, type_in, block_in, account_in, guarantee_in, fee_in,
    first_in, second_in, world_in, spread_in,
    reserve, block, capital,
    v_premium, v_charge, table, lapse, kind, block_row, account, guarantee, fee,
    first_rates, second_rates, world, spread,
    nf_all, mort_all, nf_ref, mf_ref, om_ref, lb_ref, cell, state_one, state_two,
    gb, db_one, db_two, gw, sums, first, second,
    slots_one, slots_two, kept_slots, hot, term_slots, term_out, loss_slots,
    load_sems, plan_sems, pass_sems, one_sems, total_sems, kept_sems, term_sems, loss_sems,
):
    outer_size, months_local, cells_local = nf_all.shape
    inner_size = kept_slots.shape[1]
    kept = reserve.shape[1]
    blocks = hot.shape[0]
    share = block.shape[3]
    group, group_others = peers(("inner", "cell"))
    inner_me, inner_others = peers(("inner",))
    cell_me, cell_others = peers(("cell",))
    outer_me, outer_others = peers(("outer",))
    barrier, arrivals = greet([group_others, outer_others])
    loads = [
        pltpu.make_async_copy(source, target, load_sems.at[i])
        for i, (source, target) in enumerate(
            [
                (premium, v_premium), (charge, v_charge), (mortality, mort_all.at[outer_me]),
                (table_in, table), (lapse_in, lapse), (type_in, kind), (block_in, block_row),
                (account_in, account), (guarantee_in, guarantee), (fee_in, fee),
                (first_in, first_rates), (second_in, second_rates), (world_in, world), (spread_in, spread),
            ]
        )
    ]
    for copy in loads:
        copy.start()
    finish(loads[:3])
    nf_all[outer_me] = v_premium[...] - v_charge[...]
    pl.semaphore_wait(barrier, arrivals)

    pair = inner_size % 2 == 0
    half = cells_local // 2 if pair else cells_local
    side = lax.rem(inner_me, 2) if pair else 0
    mine = pl.ds(pl.multiple_of(side * half, half), half)
    months_step = ROWS if months_local % ROWS == 0 else months_local
    plan_copies = []
    for at in range(0, months_local, months_step):
        part = []
        for d, (_, device) in enumerate(outer_others):
            for k, plan in enumerate((nf_all, mort_all)):
                rows = pl.ds(at, months_step)
                piece = plan.at[outer_me, rows, mine]
                slot = (at // months_step) * 2 * len(outer_others) + 2 * d + k
                part.append((d, plan, rows, slot, send(piece, piece, device, plan_sems, slot)))
        plan_copies.append(part)
    pass_copies = []

    def pass_on(part):
        for d, plan, rows, slot, copy in part:
            copy.wait_recv()
            if pair:
                source = lax.rem(outer_me + outer_size - 1 - d, outer_size)
                piece = plan.at[source, rows, mine]
                partner = {"inner": inner_me + 1 - 2 * side}
                pass_copies.append(send(piece, piece, partner, pass_sems, slot))

    finish(loads[3:])
    fee_row = fee[...]
    cell[0:1, :] = 1.0 - fee_row
    cell[1:2, :] = (kind[...] == 1).astype(jnp.float32)
    cell[2:3, :] = (kind[...] == 2).astype(jnp.float32)
    lapse_hot = (
        lax.broadcasted_iota(jnp.int32, (table.shape[0], cells_local), 0) == lapse[...]
    ).astype(jnp.float32)
    lb_ref[...] = lax.dot_general(
        table[...], lapse_hot, (((0,), (0,)), ((), ())),
        precision=lax.Precision.HIGHEST, preferred_element_type=jnp.float32,
    )
    world_rows = jnp.concatenate(
        [world[...], jnp.zeros((ROWS - outers, world.shape[1]), jnp.float32)], axis=0
    )
    diagonal = lax.broadcasted_iota(jnp.int32, (ROWS, outers), 0) == lax.broadcasted_iota(
        jnp.int32, (ROWS, outers), 1
    )
    spread_one = jnp.sum(jnp.where(diagonal, spread[...], 0.0), axis=1, keepdims=True)
    everything = slice(0, ROWS)
    spread_lanes(1.0 + jnp.maximum(world_rows[:, :PERIOD] - spread_one, credit_floor), gw, everything)
    fill_growth(first_rates, spread_one, gb, 0, outers, paths)
    parts = len(plan_copies)
    pass_on(plan_copies[0])
    fill_discount(first_rates, db_one)
    for part in plan_copies[1 : parts - 1]:
        pass_on(part)
    fill_discount(second_rates, db_two)
    if parts > 1:
        pass_on(plan_copies[parts - 1])
    hot[...] = (
        lax.broadcasted_iota(jnp.int32, (blocks, cells_local), 0) == block_row[...]
    ).astype(jnp.float32).astype(jnp.bfloat16)
    finish(pass_copies)
    death = 1.0 / fee_row
    for s in range(outer_size):
        rows = slice(s * months_local, (s + 1) * months_local)
        nf_ref[rows, :] = nf_all[s] * fee_row
        mf_ref[rows, :] = mort_all[s] * death
        om_ref[rows, :] = 1.0 - mort_all[s]
    plans = (nf_ref, mf_ref, om_ref, lb_ref)

    def start_one(cols):
        scale = fee[0:1, cols]
        shape = (ROWS, width)
        return (
            jnp.broadcast_to(account[0:1, cols] * scale, shape),
            jnp.ones(shape, jnp.float32),
            jnp.broadcast_to(guarantee[0:1, cols] * scale, shape),
        )

    def start_two(cols):
        return state_one[0, :, cols], state_one[1, :, cols], state_one[2, :, cols]

    year(start_one, plans, cell, gw, 0, state_one, width)
    split = -(-outers // 2)
    halves = [(low, high) for low, high in ((0, split), (split, outers)) if low < high]
    distances = len(group_others)
    one_copies = []
    for h, (low, high) in enumerate(halves):
        inner(state_one, plans, cell, gb, db_one, PERIOD, low, high, paths, sums, width)
        reduce_rows(sums, first, low, high, 1.0 / paths_all)
        slots_one[h, group] = local_totals(first, low, high)
        if h == 0:
            for part in plan_copies:
                for piece in part:
                    piece[4].wait_send()
        slot = slots_one.at[h, group]
        one_copies.append(
            [
                send(slot, slot, device, one_sems, h * distances + d)
                for d, (_, device) in enumerate(group_others)
            ]
        )
    kept_copies = []

    def send_kept(date, partial):
        for index, device in inner_others:
            kept_copies.append(
                send(
                    partial.at[pl.ds(index * kept, kept)], kept_slots.at[date, inner_me],
                    device, kept_sems, len(kept_copies),
                )
            )
        kept_slots[date, inner_me] = partial[pl.ds(inner_me * kept, kept)]

    send_kept(0, first)
    total_one = jnp.zeros((ROWS, LANES), jnp.float32)
    for h, (low, high) in enumerate(halves):
        finish(one_copies[h])
        total_one = total_one + jnp.sum(slots_one[h], axis=0)
        spread_two = (spread_one * (1.0 + jnp.tanh(total_one / cells_all)))[:, 0:1]
        spread_lanes(1.0 + jnp.maximum(world_rows[:, PERIOD:] - spread_two, credit_floor), gw, everything)
        year(start_two, plans, cell, gw, PERIOD, state_two, width)
        fill_growth(second_rates, spread_two, gb, low, high, paths)
        inner(state_two, plans, cell, gb, db_two, 2 * PERIOD, low, high, paths, sums, width)
        reduce_rows(sums, second, low, high, 1.0 / paths_all)
    slots_two[group] = local_totals(second, 0, outers)
    total_copies = [
        send(slots_two.at[group], slots_two.at[group], device, total_sems, d)
        for d, (_, device) in enumerate(group_others)
    ]
    send_kept(1, second)
    finish(kept_copies)
    held = [[jnp.sum(kept_slots[date, :, q], axis=0) for q in range(kept)] for date in range(2)]
    pieces = []
    for date in range(2):
        for q in range(kept):
            value = held[date][q]
            reserve[date, q] = value
            high = value.astype(jnp.bfloat16)
            value = value - high.astype(jnp.float32)
            middle = value.astype(jnp.bfloat16)
            low = (value - middle.astype(jnp.float32)).astype(jnp.bfloat16)
            pieces += [high.astype(jnp.float32), middle.astype(jnp.float32), low.astype(jnp.float32)]
    rows = term_slots.shape[1]
    missing = rows * 3 - len(pieces)
    stacked = jnp.concatenate(pieces + [jnp.zeros((missing, cells_local), jnp.float32)], axis=0)
    products = lax.dot_general(
        stacked.astype(jnp.bfloat16), hot[...], (((1,), (1,)), ((), ())),
        preferred_element_type=jnp.float32,
    )
    sums = [
        products[3 * i : 3 * i + 1] + products[3 * i + 1 : 3 * i + 2] + products[3 * i + 2 : 3 * i + 3]
        for i in range(rows)
    ]
    terms = jnp.concatenate(sums, axis=0)
    width = term_out.shape[2]
    for k in range(blocks // share):
        part = terms[:, k * share : (k + 1) * share]
        term_out[k] = jnp.concatenate([part, jnp.zeros((rows, width - share), jnp.float32)], axis=1)
    term_slots[cell_me] = term_out[cell_me]
    term_copies = [
        send(term_out.at[index], term_slots.at[cell_me], device, term_sems, d)
        for d, (index, device) in enumerate(cell_others)
    ]
    finish(total_copies)
    total_two = jnp.sum(slots_two[...], axis=0)
    discount = jnp.exp(-jnp.sum(world_rows[:, PERIOD:], axis=1, keepdims=True))
    loss_slots[outer_me] = (discount * total_two - total_one) / cells_all
    loss_copies = [
        send(loss_slots.at[outer_me], loss_slots.at[outer_me], device, loss_sems, d)
        for d, (_, device) in enumerate(outer_others)
    ]
    finish(term_copies)
    mine = jnp.sum(term_slots[...], axis=0)
    for date in range(2):
        for q in range(kept):
            i = date * kept + q
            block[date, q] = mine[i : i + 1, :share]
    finish(loss_copies)
    losses = jnp.concatenate([loss_slots[s, 0:outers] for s in range(loss_slots.shape[0])], axis=0)
    count = losses.shape[0]
    lane = lax.broadcasted_iota(jnp.int32, (count, LANES), 1)
    row = lax.broadcasted_iota(jnp.int32, (count, LANES), 0)
    across = jnp.sum(jnp.where(lane == row, losses, 0.0), axis=0, keepdims=True)
    ahead = ((across > losses) | ((across == losses) & (lane < row))) & (lane < count)
    rank = jnp.sum(jnp.where(ahead, 1.0, 0.0), axis=1, keepdims=True)
    top = count // 4
    taken = jnp.sum(jnp.where(rank < top, losses, 0.0), axis=0, keepdims=True) / top
    capital[...] = taken


def body(
    premium, charge, mortality, lapse_table, lapse_index, guarantee_type, block_index,
    account_start, guarantee_start, fee_rate, first_rates, second_rates, world_rates, spread,
):
    months_local, cells_local = premium.shape
    outer_size, inner_size, cell_size = (lax.axis_size(axis) for axis in ("outer", "inner", "cell"))
    months = months_local * outer_size
    group_size = inner_size * cell_size
    outers, paths = first_rates.shape[:2]
    paths_all = paths * inner_size
    cells_all = cells_local * cell_size
    width = 4 * LANES
    kept = outers // inner_size
    blocks = 4 * cells_all // BLOCK
    share = blocks // cell_size
    wide = -(-share // LANES) * LANES
    term_rows = -(-2 * kept // ROWS) * ROWS
    f32, i32 = jnp.float32, jnp.int32
    shape = jax.ShapeDtypeStruct

    def row(x):
        return x.reshape(1, -1)

    def buffer(*dims, dtype=f32):
        return pltpu.VMEM(dims, dtype)

    def sems(count):
        return pltpu.SemaphoreType.DMA((2, max(count, 1)))

    chunks = months_local // ROWS if months_local % ROWS == 0 else 1
    plan_count = 2 * chunks * (outer_size - 1)
    plan = buffer(months, cells_local)
    gathered = buffer(outer_size, months_local, cells_local)
    line, code = buffer(1, cells_local), buffer(1, cells_local, dtype=i32)
    total_rows = outers * paths
    first_months, second_months = first_rates.shape[2], second_rates.shape[2]
    operands = (
        premium, charge, mortality, lapse_table, row(lapse_index), row(guarantee_type), row(block_index),
        row(account_start), row(guarantee_start), row(fee_rate),
        first_rates.reshape(total_rows, -1), second_rates.reshape(total_rows, -1), world_rates, row(spread),
    )
    reserve, block, capital = pl.pallas_call(
        functools.partial(whole_kernel, outers, paths, paths_all, cells_all, width),
        out_shape=[
            shape((2, kept, 1, cells_local), f32), shape((2, kept, 1, share), f32), shape((1, LANES), f32),
        ],
        in_specs=[pl.BlockSpec(memory_space=pl.ANY)] * len(operands),
        out_specs=[VMEM] * 3,
        scratch_shapes=[
            buffer(months_local, cells_local), buffer(months_local, cells_local), buffer(*lapse_table.shape),
            code, code, code, line, line, line,
            buffer(total_rows, first_months), buffer(total_rows, second_months),
            buffer(*world_rates.shape), buffer(1, outers),
            gathered, gathered, plan, plan, plan, plan, buffer(ROWS, cells_local),
            buffer(3, ROWS, cells_local), buffer(3, ROWS, cells_local),
            buffer(first_months, total_rows, LANES), buffer(first_months, total_rows, LANES),
            buffer(second_months, total_rows, LANES), buffer(PERIOD, ROWS, LANES),
            buffer(outers, ROWS, cells_local), buffer(outers, 1, cells_local), buffer(outers, 1, cells_local),
            buffer(2, group_size, ROWS, LANES), buffer(group_size, ROWS, LANES),
            buffer(2, inner_size, kept, 1, cells_local), buffer(blocks, cells_local, dtype=jnp.bfloat16),
            buffer(cell_size, term_rows, wide), buffer(cell_size, term_rows, wide),
            buffer(outer_size, ROWS, LANES),
            pltpu.SemaphoreType.DMA((len(operands),)), sems(plan_count), sems(plan_count),
            sems(2 * (group_size - 1)), sems(group_size - 1), sems(2 * (inner_size - 1)),
            sems(cell_size - 1), sems(outer_size - 1),
        ],
        compiler_params=pltpu.CompilerParams(
            collective_id=0, has_side_effects=True, vmem_limit_bytes=60 * 2**20
        ),
    )(*operands)
    return (
        reserve.reshape(2, kept, cells_local),
        block.reshape(2, kept, share),
        capital[0, :1],
    )


def solution(mesh):
    placed = (
        P("outer", "cell"), P("outer", "cell"), P("outer", "cell"), P(), P("cell"), P("cell"), P("cell"),
        P("cell"), P("cell"), P("cell"), P("outer", "inner", None), P("outer", "inner", None),
        P("outer", None), P("outer"),
    )
    return jax.shard_map(
        body,
        mesh=mesh,
        in_specs=placed,
        out_specs=(P(None, ("outer", "inner"), "cell"), P(None, ("outer", "inner"), "cell"), P()),
        check_vma=False,
    )
```

profile of v0, /device:TPU:0, one launch (start us, length us, event | category | flops | bytes accessed | tf_op | source)
XLA Modules:
  0.0 46.8 jit_solution(3693344660516386083)
XLA Ops:
  0.6 43.0 %shard_map.157 = (f32[2,1,1,2048]{3,2,1,0:T(1,128)}, f32[2,1,1,64]{3,2,1,0:T(1,128)}, f32[1,128]{1,0:T(1,128)}) custom-call(f32[24,2048]{1,0:T(8,128)} %premium.1, f32[24,2048]{1,0:T(8,128)} %charge.1, f32[24,2048]{1,0:T(8,128)} %mortality.1, f32[16,48]{1,0:T(8,128)} %table_in.1, s32[1,2048]{1,0:T(1,128)} %bitcast.18, s32[1,2048]{1,0:T(1,128)} %bitcast.19, ...), custom_call_target="tpu_custom_call" | custom-call | tf_op jit(solution)/shard_map/pallas_call | solution.py:469
  43.7 0.0 copy-start
  43.7 1.3 %copy.21 = f32[2,1,2048]{2,1,0:T(1,128)} copy(f32[2,1,2048]{2,1,0:T(1,128)} %bitcast.17) | data formatting | bytes 32768
  45.0 0.0 copy-done
  45.0 0.0 copy-start.1
  45.0 0.6 %copy.22 = f32[2,1,64]{2,1,0:T(1,128)} copy(f32[2,1,64]{2,1,0:T(1,128)S(1)} %bitcast.24) | data formatting | bytes 1024
  45.6 0.0 copy-done.1
Async XLA Ops:
  43.7 1.3 %copy-start = (f32[2,1,1,64]{3,2,1,0:T(1,128)S(1)}, f32[2,1,1,64]{3,2,1,0:T(1,128)}, u32[]{:S(2)}) copy-start(f32[2,1,1,64]{3,2,1,0:T(1,128)} %get-tuple-element.7) | copy-start | bytes 1540
  45.0 0.6 %copy-start.1 = (f32[1,128]{1,0:T(1,128)S(1)}, f32[1,128]{1,0:T(1,128)}, u32[]{:S(2)}) copy-start(f32[1,128]{1,0:T(1,128)} %get-tuple-element.8) | copy-start | bytes 1540
where the time goes:
time: 47.1 us; the launch traced here: 46.8 us
  Pallas kernels  43 us (91%)
  local copies, waits for them, and re-layouts  1.94 us (4%)
  between operations  1.82 us (4%)
    pallas_call x1, Pallas kernels, body(): pl.pallas_call(functools.partial(whole_kernel, outers, paths, paths_all,...  43 us
    unnamed x6, local copies, waits for them, and re-layouts  1.94 us

commit v1 on v0

--- a/solution.py
+++ b/solution.py
@@ -170,6 +170,25 @@
     return barrier, count
 
 
+def beside(me, size, act):
+    @pl.when(me > 0)
+    def _():
+        act({"cell": me - 1})
+
+    @pl.when(me < size - 1)
+    def _():
+        act({"cell": me + 1})
+
+    return (me > 0).astype(jnp.int32) + (me < size - 1).astype(jnp.int32)
+
+
+def signal_to(sem):
+    def act(device):
+        pl.semaphore_signal(sem, inc=1, device_id=device, device_id_type=pl.DeviceIdType.MESH)
+
+    return act
+
+
 def send(source, target, device, sems, at):
     copy = pltpu.make_async_remote_copy(
         src_ref=source,
@@ -207,7 +226,7 @@
     nf_all, mort_all, nf_ref, mf_ref, om_ref, lb_ref, cell, state_one, state_two,
     gb, db_one, db_two, gw, sums, first, second,
     slots_one, slots_two, kept_slots, hot, term_slots, term_out, loss_slots,
-    load_sems, plan_sems, pass_sems, one_sems, total_sems, kept_sems, term_sems, loss_sems,
+    load_sems, plan_sems, pass_sems, one_sems, total_sems, kept_sems, term_sems, loss_sems, relay_sems,
 ):
     outer_size, months_local, cells_local = nf_all.shape
     inner_size = kept_slots.shape[1]
@@ -218,7 +237,9 @@
     inner_me, inner_others = peers(("inner",))
     cell_me, cell_others = peers(("cell",))
     outer_me, outer_others = peers(("outer",))
-    barrier, arrivals = greet([group_others, outer_others])
+    barrier, arrivals = greet([inner_others, outer_others])
+    cell_size = term_slots.shape[0]
+    arrivals = arrivals + beside(cell_me, cell_size, signal_to(barrier))
     loads = [
         pltpu.make_async_copy(source, target, load_sems.at[i])
         for i, (source, target) in enumerate(
@@ -262,6 +283,8 @@
                 partner = {"inner": inner_me + 1 - 2 * side}
                 pass_copies.append(send(piece, piece, partner, pass_sems, slot))
 
+    rounds = relay_sems.shape[0]
+    near = beside(cell_me, cell_size, signal_to(relay_sems.at[0]))
     finish(loads[3:])
     fee_row = fee[...]
     cell[0:1, :] = 1.0 - fee_row
@@ -316,6 +339,9 @@
     def start_two(cols):
         return state_one[0, :, cols], state_one[1, :, cols], state_one[2, :, cols]
 
+    for r in range(1, rounds):
+        pl.semaphore_wait(relay_sems.at[r - 1], near)
+        beside(cell_me, cell_size, signal_to(relay_sems.at[r]))
     year(start_one, plans, cell, gw, 0, state_one, width)
     split = -(-outers // 2)
     halves = [(low, high) for low, high in ((0, split), (split, outers)) if low < high]
@@ -329,6 +355,7 @@
             for part in plan_copies:
                 for piece in part:
                     piece[4].wait_send()
+            pl.semaphore_wait(relay_sems.at[rounds - 1], near)
         slot = slots_one.at[h, group]
         one_copies.append(
             [
@@ -489,7 +516,7 @@
             buffer(outer_size, ROWS, LANES),
             pltpu.SemaphoreType.DMA((len(operands),)), sems(plan_count), sems(plan_count),
             sems(2 * (group_size - 1)), sems(group_size - 1), sems(2 * (inner_size - 1)),
-            sems(cell_size - 1), sems(outer_size - 1),
+            sems(cell_size - 1), sems(outer_size - 1), pltpu.SemaphoreType.REGULAR((max(cell_size - 1, 1),)),
         ],
         compiler_params=pltpu.CompilerParams(
             collective_id=0, has_side_effects=True, vmem_limit_bytes=60 * 2**20

time: 47.1 us -> 46 us (0.977)
  Pallas kernels: 43 us -> 42 us
    pallas_call x1, Pallas kernels: 43 us -> 42 us  [body(): pl.pallas_call(functools.partial(whole_kernel, outers, paths, paths_all,...]
where the time goes in v1:
time: 46 us; the launch traced here: 45.7 us
  Pallas kernels  42 us (91%)
  local copies, waits for them, and re-layouts  1.94 us (4%)
  between operations  1.82 us (4%)
    pallas_call x1, Pallas kernels, body(): pl.pallas_call(functools.partial(whole_kernel, outers, paths, paths_all,...  42 us
    unnamed x6, local copies, waits for them, and re-layouts  1.94 us

profile of v1, /device:TPU:0, one launch (start us, length us, event | category | flops | bytes accessed | tf_op | source)
XLA Modules:
  0.0 45.7 jit_solution(10262807015079991137)
XLA Ops:
  0.6 42.0 %shard_map.157 = (f32[2,1,1,2048]{3,2,1,0:T(1,128)}, f32[2,1,1,64]{3,2,1,0:T(1,128)}, f32[1,128]{1,0:T(1,128)}) custom-call(f32[24,2048]{1,0:T(8,128)} %premium.1, f32[24,2048]{1,0:T(8,128)} %charge.1, f32[24,2048]{1,0:T(8,128)} %mortality.1, f32[16,48]{1,0:T(8,128)} %table_in.1, s32[1,2048]{1,0:T(1,128)} %bitcast.18, s32[1,2048]{1,0:T(1,128)} %bitcast.19, ...), custom_call_target="tpu_custom_call" | custom-call | tf_op jit(solution)/shard_map/pallas_call | solution.py:496
  42.6 0.0 copy-start
  42.6 1.3 %copy.21 = f32[2,1,2048]{2,1,0:T(1,128)} copy(f32[2,1,2048]{2,1,0:T(1,128)} %bitcast.17) | data formatting | bytes 32768
  44.0 0.0 copy-done
  44.0 0.0 copy-start.1
  44.0 0.6 %copy.22 = f32[2,1,64]{2,1,0:T(1,128)} copy(f32[2,1,64]{2,1,0:T(1,128)S(1)} %bitcast.24) | data formatting | bytes 1024
  44.5 0.0 copy-done.1
Async XLA Ops:
  42.6 1.3 %copy-start = (f32[2,1,1,64]{3,2,1,0:T(1,128)S(1)}, f32[2,1,1,64]{3,2,1,0:T(1,128)}, u32[]{:S(2)}) copy-start(f32[2,1,1,64]{3,2,1,0:T(1,128)} %get-tuple-element.7) | copy-start | bytes 1540
  44.0 0.6 %copy-start.1 = (f32[1,128]{1,0:T(1,128)S(1)}, f32[1,128]{1,0:T(1,128)}, u32[]{:S(2)}) copy-start(f32[1,128]{1,0:T(1,128)} %get-tuple-element.8) | copy-start | bytes 1540

commit v2 on v1

--- a/solution.py
+++ b/solution.py
@@ -10,6 +10,7 @@
 BLOCK = 128
 LANES = 128
 ROWS = 8
+DIRECT = 32
 
 credit_floor = 0.001
 rollup_growth = 0.05
@@ -230,6 +231,7 @@
 ):
     outer_size, months_local, cells_local = nf_all.shape
     inner_size = kept_slots.shape[1]
+    cell_size = term_out.shape[0]
     kept = reserve.shape[1]
     blocks = hot.shape[0]
     share = block.shape[3]
@@ -237,8 +239,9 @@
     inner_me, inner_others = peers(("inner",))
     cell_me, cell_others = peers(("cell",))
     outer_me, outer_others = peers(("outer",))
+    direct = slots_two.shape[0] > inner_size * cell_size
+    all_me, all_others = peers(("outer", "inner", "cell")) if direct else (group, group_others)
     barrier, arrivals = greet([inner_others, outer_others])
-    cell_size = term_slots.shape[0]
     arrivals = arrivals + beside(cell_me, cell_size, signal_to(barrier))
     loads = [
         pltpu.make_async_copy(source, target, load_sems.at[i])
@@ -386,70 +389,86 @@
         fill_growth(second_rates, spread_two, gb, low, high, paths)
         inner(state_two, plans, cell, gb, db_two, 2 * PERIOD, low, high, paths, sums, width)
         reduce_rows(sums, second, low, high, 1.0 / paths_all)
-    slots_two[group] = local_totals(second, 0, outers)
+    discount = jnp.exp(-jnp.sum(world_rows[:, PERIOD:], axis=1, keepdims=True))
+    mine_one = slots_one[0, group]
+    for h in range(1, len(halves)):
+        mine_one = mine_one + slots_one[h, group]
+    mine_loss = (discount * local_totals(second, 0, outers) - mine_one) / cells_all
+    own = lax.broadcasted_iota(jnp.int32, (ROWS, LANES), 0)
+    own_lane = lax.broadcasted_iota(jnp.int32, (ROWS, LANES), 1) - outer_me * outers
+    mine_loss = jnp.where((own == own_lane) & (own < outers), mine_loss, 0.0)
+    place, others = (all_me, all_others) if direct else (group, group_others)
+    slots_two[place] = jnp.sum(mine_loss, axis=0, keepdims=True)
     total_copies = [
-        send(slots_two.at[group], slots_two.at[group], device, total_sems, d)
-        for d, (_, device) in enumerate(group_others)
+        send(slots_two.at[place], slots_two.at[place], device, total_sems, d)
+        for d, (_, device) in enumerate(others)
     ]
     send_kept(1, second)
-    finish(kept_copies)
-    held = [[jnp.sum(kept_slots[date, :, q], axis=0) for q in range(kept)] for date in range(2)]
-    pieces = []
-    for date in range(2):
-        for q in range(kept):
-            value = held[date][q]
-            reserve[date, q] = value
-            high = value.astype(jnp.bfloat16)
-            value = value - high.astype(jnp.float32)
-            middle = value.astype(jnp.bfloat16)
-            low = (value - middle.astype(jnp.float32)).astype(jnp.bfloat16)
-            pieces += [high.astype(jnp.float32), middle.astype(jnp.float32), low.astype(jnp.float32)]
-    rows = term_slots.shape[1]
-    missing = rows * 3 - len(pieces)
-    stacked = jnp.concatenate(pieces + [jnp.zeros((missing, cells_local), jnp.float32)], axis=0)
+    step = -(-outers // ROWS) * ROWS
+    lines = 2 * step
+    line = lax.broadcasted_iota(jnp.int32, (step, cells_local), 0)
+    values = []
+    for partial in (first, second):
+        value = jnp.zeros((step, cells_local), jnp.float32)
+        for o in range(outers):
+            value = jnp.where(line == o, jnp.broadcast_to(partial[o], value.shape), value)
+        values.append(value)
+    value = jnp.concatenate(values, axis=0)
+    high = value.astype(jnp.bfloat16).astype(jnp.float32)
+    value = value - high
+    middle = value.astype(jnp.bfloat16).astype(jnp.float32)
+    stacked = jnp.concatenate([high, middle, value - middle], axis=0)
     products = lax.dot_general(
         stacked.astype(jnp.bfloat16), hot[...], (((1,), (1,)), ((), ())),
         preferred_element_type=jnp.float32,
     )
-    sums = [
-        products[3 * i : 3 * i + 1] + products[3 * i + 1 : 3 * i + 2] + products[3 * i + 2 : 3 * i + 3]
-        for i in range(rows)
+    terms = products[:lines] + products[lines : 2 * lines] + products[2 * lines :]
+    width = term_out.shape[3]
+    for k in range(cell_size):
+        spot = slice(k * share, (k + 1) * share)
+        part = [terms[:step, spot], terms[step:, spot]]
+        if width > 2 * share:
+            part.append(jnp.zeros((step, width - 2 * share), jnp.float32))
+        part = jnp.concatenate(part, axis=1)
+        for o in range(outers):
+            term_out[k, o] = part[o : o + 1]
+    term_slots[group] = term_out[cell_me, pl.ds(inner_me * kept, kept)]
+    term_copies = [
+        send(
+            term_out.at[lax.rem(index, cell_size), pl.ds(lax.div(index, cell_size) * kept, kept)],
+            term_slots.at[group], device, term_sems, d,
+        )
+        for d, (index, device) in enumerate(group_others)
     ]
-    terms = jnp.concatenate(sums, axis=0)
-    width = term_out.shape[2]
-    for k in range(blocks // share):
-        part = terms[:, k * share : (k + 1) * share]
-        term_out[k] = jnp.concatenate([part, jnp.zeros((rows, width - share), jnp.float32)], axis=1)
-    term_slots[cell_me] = term_out[cell_me]
-    term_copies = [
-        send(term_out.at[index], term_slots.at[cell_me], device, term_sems, d)
-        for d, (index, device) in enumerate(cell_others)
-    ]
-    finish(total_copies)
-    total_two = jnp.sum(slots_two[...], axis=0)
-    discount = jnp.exp(-jnp.sum(world_rows[:, PERIOD:], axis=1, keepdims=True))
-    loss_slots[outer_me] = (discount * total_two - total_one) / cells_all
-    loss_copies = [
-        send(loss_slots.at[outer_me], loss_slots.at[outer_me], device, loss_sems, d)
-        for d, (_, device) in enumerate(outer_others)
-    ]
-    finish(term_copies)
-    mine = jnp.sum(term_slots[...], axis=0)
+    finish(kept_copies)
     for date in range(2):
         for q in range(kept):
-            i = date * kept + q
-            block[date, q] = mine[i : i + 1, :share]
-    finish(loss_copies)
-    losses = jnp.concatenate([loss_slots[s, 0:outers] for s in range(loss_slots.shape[0])], axis=0)
-    count = losses.shape[0]
+            reserve[date, q] = jnp.sum(kept_slots[date, :, q], axis=0)
+    finish(term_copies)
+    for q in range(kept):
+        mine = jnp.sum(term_slots[:, q], axis=0)
+        for date in range(2):
+            block[date, q] = mine[:, date * share : (date + 1) * share]
+    finish(total_copies)
+    across = jnp.sum(slots_two[...], axis=0)
+    if not direct:
+        loss_slots[outer_me] = across
+        finish(
+            [
+                send(loss_slots.at[outer_me], loss_slots.at[outer_me], device, loss_sems, d)
+                for d, (_, device) in enumerate(outer_others)
+            ]
+        )
+        across = jnp.sum(loss_slots[...], axis=0)
+    count = outers * outer_size
     lane = lax.broadcasted_iota(jnp.int32, (count, LANES), 1)
     row = lax.broadcasted_iota(jnp.int32, (count, LANES), 0)
-    across = jnp.sum(jnp.where(lane == row, losses, 0.0), axis=0, keepdims=True)
+    losses = jnp.sum(jnp.where(lane == row, across, 0.0), axis=1, keepdims=True)
     ahead = ((across > losses) | ((across == losses) & (lane < row))) & (lane < count)
     rank = jnp.sum(jnp.where(ahead, 1.0, 0.0), axis=1, keepdims=True)
     top = count // 4
     taken = jnp.sum(jnp.where(rank < top, losses, 0.0), axis=0, keepdims=True) / top
-    capital[...] = taken
+    capital[...] = jnp.broadcast_to(taken, capital.shape)
 
 
 def body(
@@ -467,8 +486,9 @@
     kept = outers // inner_size
     blocks = 4 * cells_all // BLOCK
     share = blocks // cell_size
-    wide = -(-share // LANES) * LANES
-    term_rows = -(-2 * kept // ROWS) * ROWS
+    wide = -(-2 * share // LANES) * LANES
+    everyone = outer_size * group_size
+    wide_count = everyone if everyone <= DIRECT else group_size
     f32, i32 = jnp.float32, jnp.int32
     shape = jax.ShapeDtypeStruct
 
@@ -510,18 +530,18 @@
             buffer(first_months, total_rows, LANES), buffer(first_months, total_rows, LANES),
             buffer(second_months, total_rows, LANES), buffer(PERIOD, ROWS, LANES),
             buffer(outers, ROWS, cells_local), buffer(outers, 1, cells_local), buffer(outers, 1, cells_local),
-            buffer(2, group_size, ROWS, LANES), buffer(group_size, ROWS, LANES),
+            buffer(2, group_size, ROWS, LANES), buffer(wide_count, 1, LANES),
             buffer(2, inner_size, kept, 1, cells_local), buffer(blocks, cells_local, dtype=jnp.bfloat16),
-            buffer(cell_size, term_rows, wide), buffer(cell_size, term_rows, wide),
-            buffer(outer_size, ROWS, LANES),
+            buffer(group_size, kept, 1, wide), buffer(cell_size, outers, 1, wide),
+            buffer(outer_size, 1, LANES),
             pltpu.SemaphoreType.DMA((len(operands),)), sems(plan_count), sems(plan_count),
-            sems(2 * (group_size - 1)), sems(group_size - 1), sems(2 * (inner_size - 1)),
-            sems(cell_size - 1), sems(outer_size - 1), pltpu.SemaphoreType.REGULAR((max(cell_size - 1, 1),)),
+            sems(2 * (group_size - 1)), sems(wide_count - 1), sems(2 * (inner_size - 1)),
+            sems(group_size - 1), sems(outer_size - 1), pltpu.SemaphoreType.REGULAR((max(cell_size - 1, 1),)),
         ],
         compiler_params=pltpu.CompilerParams(
-            collective_id=0, has_side_effects=True, vmem_limit_bytes=60 * 2**20
+            collective_id=0, has_side_effects=True, vmem_limit_bytes=24*2**20
         ),
-    )(*operands)
+    )(*[pltpu.with_memory_space_constraint(x, pltpu.HBM) for x in operands])
     return (
         reserve.reshape(2, kept, cells_local),
         block.reshape(2, kept, share),

time: 46 us -> 43.5 us (0.946)
  Pallas kernels: 42 us -> 40.4 us
  local copies, waits for them, and re-layouts: 1.94 us -> 1.17 us
    pallas_call x1, Pallas kernels: 42 us -> 40.4 us  [body(): pl.pallas_call(functools.partial(whole_kernel, outers, paths, paths_all,...]
    unnamed x6 -> x2, local copies, waits for them, and re-layouts: 1.94 us -> 1.17 us
where the time goes in v2:
time: 43.5 us; the launch traced here: 43.3 us
  Pallas kernels  40.4 us (93%)
  between operations  1.81 us (4%)
  local copies, waits for them, and re-layouts  1.17 us (3%)
    pallas_call x1, Pallas kernels, body(): pl.pallas_call(functools.partial(whole_kernel, outers, paths, paths_all,...  40.4 us
    unnamed x2, local copies, waits for them, and re-layouts  1.17 us

profile of v2, /device:TPU:0, one launch (start us, length us, event | category | flops | bytes accessed | tf_op | source)
XLA Modules:
  0.0 43.3 jit_solution(258143780170022983)
XLA Ops:
  0.6 40.4 %shard_map.157 = (f32[2,1,1,2048]{3,2,1,0:T(1,128)S(1)}, f32[2,1,1,64]{3,2,1,0:T(1,128)S(1)}, f32[1,128]{1,0:T(1,128)S(1)}) custom-call(f32[24,2048]{1,0:T(8,128)} %premium.1, f32[24,2048]{1,0:T(8,128)} %charge.1, f32[24,2048]{1,0:T(8,128)} %mortality.1, f32[16,48]{1,0:T(8,128)} %table_in.1, s32[1,2048]{1,0:T(1,128)} %bitcast.20, s32[1,2048]{1,0:T(1,128)} %bitcast.21, ...), custom_call_target="tpu_custom_call" | custom-call | tf_op jit(solution)/shard_map/pallas_call | solution.py:516
  41.0 0.6 %copy.21 = f32[2,1,2048]{2,1,0:T(1,128)} copy(f32[2,1,2048]{2,1,0:T(1,128)S(1)} %bitcast.15) | data formatting | bytes 32768
  41.6 0.6 %copy.22 = f32[2,1,64]{2,1,0:T(1,128)} copy(f32[2,1,64]{2,1,0:T(1,128)S(1)} %bitcast.16) | data formatting | bytes 1024

commit v3 on v2

--- a/solution.py
+++ b/solution.py
@@ -287,6 +287,12 @@
                 pass_copies.append(send(piece, piece, partner, pass_sems, slot))
 
     rounds = relay_sems.shape[0]
+
+    def relay(low, high):
+        for r in range(low, min(high, rounds)):
+            pl.semaphore_wait(relay_sems.at[r - 1], near)
+            beside(cell_me, cell_size, signal_to(relay_sems.at[r]))
+
     near = beside(cell_me, cell_size, signal_to(relay_sems.at[0]))
     finish(loads[3:])
     fee_row = fee[...]
@@ -312,6 +318,7 @@
     fill_growth(first_rates, spread_one, gb, 0, outers, paths)
     parts = len(plan_copies)
     pass_on(plan_copies[0])
+    relay(1, 2)
     fill_discount(first_rates, db_one)
     for part in plan_copies[1 : parts - 1]:
         pass_on(part)
@@ -321,6 +328,7 @@
     hot[...] = (
         lax.broadcasted_iota(jnp.int32, (blocks, cells_local), 0) == block_row[...]
     ).astype(jnp.float32).astype(jnp.bfloat16)
+    relay(2, rounds)
     finish(pass_copies)
     death = 1.0 / fee_row
     for s in range(outer_size):
@@ -342,9 +350,6 @@
     def start_two(cols):
         return state_one[0, :, cols], state_one[1, :, cols], state_one[2, :, cols]
 
-    for r in range(1, rounds):
-        pl.semaphore_wait(relay_sems.at[r - 1], near)
-        beside(cell_me, cell_size, signal_to(relay_sems.at[r]))
     year(start_one, plans, cell, gw, 0, state_one, width)
     split = -(-outers // 2)
     halves = [(low, high) for low, high in ((0, split), (split, outers)) if low < high]
@@ -471,6 +476,19 @@
     capital[...] = jnp.broadcast_to(taken, capital.shape)
 
 
+def settle(reserve, block, capital, reserve_out, block_out, capital_out, single, sems):
+    single[...] = capital[:, :1]
+    copies = [
+        pltpu.make_async_copy(source, target, sems.at[i])
+        for i, (source, target) in enumerate(
+            [(reserve, reserve_out), (block, block_out), (single, capital_out)]
+        )
+    ]
+    for copy in copies:
+        copy.start()
+    finish(copies)
+
+
 def body(
     premium, charge, mortality, lapse_table, lapse_index, guarantee_type, block_index,
     account_start, guarantee_start, fee_rate, first_rates, second_rates, world_rates, spread,
@@ -542,10 +560,18 @@
             collective_id=0, has_side_effects=True, vmem_limit_bytes=24*2**20
         ),
     )(*[pltpu.with_memory_space_constraint(x, pltpu.HBM) for x in operands])
+    reserve, block, capital = pl.pallas_call(
+        settle,
+        out_shape=[shape(reserve.shape, f32), shape(block.shape, f32), shape((1, 1), f32)],
+        in_specs=[VMEM] * 3,
+        out_specs=[pl.BlockSpec(memory_space=pltpu.HBM)] * 3,
+        scratch_shapes=[buffer(1, 1), pltpu.SemaphoreType.DMA((3,))],
+        compiler_params=pltpu.CompilerParams(vmem_limit_bytes=2**20),
+    )(reserve, block, capital)
     return (
         reserve.reshape(2, kept, cells_local),
         block.reshape(2, kept, share),
-        capital[0, :1],
+        capital.reshape(1),
     )
 
 

time: 43.5 us -> 41.2 us (0.947)
  local copies, waits for them, and re-layouts: 1.17 us -> 0 us
  between operations: 1.81 us -> 0.64 us
    unnamed x2 -> x0, local copies, waits for them, and re-layouts: 1.17 us -> none
    pallas_call x0 -> x1, Pallas kernels: none -> 0.64 us  [body(): pl.pallas_call(settle, out_shape=[shape(reserve.shape, f32), shape(block....]
    pallas_call x1, Pallas kernels: 40.4 us -> 39.8 us  [body(): pl.pallas_call(functools.partial(whole_kernel, outers, paths, paths_all,...]
where the time goes in v3:
time: 41.2 us; the launch traced here: 41 us
  Pallas kernels  40.4 us (98%)
  between operations  0.64 us (2%)
    pallas_call x1, Pallas kernels, body(): pl.pallas_call(functools.partial(whole_kernel, outers, paths, paths_all,...  39.8 us

profile of v3, /device:TPU:0, one launch (start us, length us, event | category | flops | bytes accessed | tf_op | source)
XLA Modules:
  0.0 41.0 jit_solution(14248365454216242117)
XLA Ops:
  0.6 39.8 %shard_map.157 = (f32[2,1,1,2048]{3,2,1,0:T(1,128)S(1)}, f32[2,1,1,64]{3,2,1,0:T(1,128)S(1)}, f32[1,128]{1,0:T(1,128)S(1)}) custom-call(f32[24,2048]{1,0:T(8,128)} %premium.1, f32[24,2048]{1,0:T(8,128)} %charge.1, f32[24,2048]{1,0:T(8,128)} %mortality.1, f32[16,48]{1,0:T(8,128)} %table_in.1, s32[1,2048]{1,0:T(1,128)} %bitcast.16, s32[1,2048]{1,0:T(1,128)} %bitcast.17, ...), custom_call_target="tpu_custom_call" | custom-call | tf_op jit(solution)/shard_map/pallas_call | solution.py:534
  40.4 0.6 %shard_map.158 = (f32[2,1,1,2048]{3,2,1,0:T(1,128)}, f32[2,1,1,64]{3,2,1,0:T(1,128)}, f32[1,1]{1,0:T(1,128)}) custom-call(f32[2,1,1,2048]{3,2,1,0:T(1,128)S(1)} %get-tuple-element.9.reserve, f32[2,1,1,64]{3,2,1,0:T(1,128)S(1)} %get-tuple-element.10.block, f32[1,128]{1,0:T(1,128)S(1)} %get-tuple-element.11.capital), custom_call_target="tpu_custom_call" | custom-call | tf_op jit(solution)/shard_map/pallas_call | solution.py:563

commit v4 on v3

--- a/solution.py
+++ b/solution.py
@@ -53,9 +53,8 @@
         target[m, rows, :] = jnp.broadcast_to(values[:, m : m + 1], (values.shape[0], LANES))
 
 
-def year(start, plans, cell, growth_lanes, first_month, state, width):
+def year(start, plans, cell, growth_lanes, first_month, state, width, begin, end):
     nf_ref, mf_ref, om_ref, lb_ref = plans
-    total = nf_ref.shape[1]
     repeat = width // LANES
 
     def chunk(j, _):
@@ -80,19 +79,18 @@
         state[2, :, cols] = anniversary(account, guarantee, ratchet, rollup)
         return 0
 
-    lax.fori_loop(0, total // width, chunk, 0)
-
-
-def inner(state, plans, cell, gb, db, first_month, low, high, paths, sums, width):
+    lax.fori_loop(begin, end, chunk, 0)
+
+
+def inner(state, plans, cell, gb, db, first_month, low, high, paths, sums, width, begin, end):
     nf_ref, mf_ref, om_ref, lb_ref = plans
-    total = nf_ref.shape[1]
     repeat = width // LANES
     months = db.shape[0]
     groups = paths // ROWS
-    chunks = total // width
+    chunks = end - begin
 
     def block(step, _):
-        o, j = low + step // chunks, step % chunks
+        o, j = low + step // chunks, begin + step % chunks
         cols = pl.ds(pl.multiple_of(j * width, width), width)
         keep, ratchet, rollup = cell[0:1, cols], cell[1:2, cols], cell[2:3, cols]
         shape = (ROWS, width)
@@ -261,30 +259,31 @@
     pl.semaphore_wait(barrier, arrivals)
 
     pair = inner_size % 2 == 0
-    half = cells_local // 2 if pair else cells_local
+    chunks = cells_local // width
+    part = width // 2 if pair else width
     side = lax.rem(inner_me, 2) if pair else 0
-    mine = pl.ds(pl.multiple_of(side * half, half), half)
-    months_step = ROWS if months_local % ROWS == 0 else months_local
     plan_copies = []
-    for at in range(0, months_local, months_step):
-        part = []
+    for j in range(chunks):
+        mine = pl.ds(pl.multiple_of(j * width + side * part, part), part)
+        copies = []
         for d, (_, device) in enumerate(outer_others):
             for k, plan in enumerate((nf_all, mort_all)):
-                rows = pl.ds(at, months_step)
-                piece = plan.at[outer_me, rows, mine]
-                slot = (at // months_step) * 2 * len(outer_others) + 2 * d + k
-                part.append((d, plan, rows, slot, send(piece, piece, device, plan_sems, slot)))
-        plan_copies.append(part)
+                piece = plan.at[outer_me, :, mine]
+                slot = (j * len(outer_others) + d) * 2 + k
+                copies.append((d, plan, mine, slot, send(piece, piece, device, plan_sems, slot)))
+        plan_copies.append(copies)
     pass_copies = []
 
-    def pass_on(part):
-        for d, plan, rows, slot, copy in part:
+    def pass_on(j):
+        copies = []
+        for d, plan, mine, slot, copy in plan_copies[j]:
             copy.wait_recv()
             if pair:
                 source = lax.rem(outer_me + outer_size - 1 - d, outer_size)
-                piece = plan.at[source, rows, mine]
+                piece = plan.at[source, :, mine]
                 partner = {"inner": inner_me + 1 - 2 * side}
-                pass_copies.append(send(piece, piece, partner, pass_sems, slot))
+                copies.append(send(piece, piece, partner, pass_sems, slot))
+        pass_copies.append(copies)
 
     rounds = relay_sems.shape[0]
 
@@ -316,27 +315,27 @@
     everything = slice(0, ROWS)
     spread_lanes(1.0 + jnp.maximum(world_rows[:, :PERIOD] - spread_one, credit_floor), gw, everything)
     fill_growth(first_rates, spread_one, gb, 0, outers, paths)
-    parts = len(plan_copies)
-    pass_on(plan_copies[0])
-    relay(1, 2)
     fill_discount(first_rates, db_one)
-    for part in plan_copies[1 : parts - 1]:
-        pass_on(part)
     fill_discount(second_rates, db_two)
-    if parts > 1:
-        pass_on(plan_copies[parts - 1])
     hot[...] = (
         lax.broadcasted_iota(jnp.int32, (blocks, cells_local), 0) == block_row[...]
     ).astype(jnp.float32).astype(jnp.bfloat16)
-    relay(2, rounds)
-    finish(pass_copies)
+    ahead = min(2, chunks)
+    for j in range(ahead):
+        pass_on(j)
+    relay(1, 2)
     death = 1.0 / fee_row
-    for s in range(outer_size):
-        rows = slice(s * months_local, (s + 1) * months_local)
-        nf_ref[rows, :] = nf_all[s] * fee_row
-        mf_ref[rows, :] = mort_all[s] * death
-        om_ref[rows, :] = 1.0 - mort_all[s]
     plans = (nf_ref, mf_ref, om_ref, lb_ref)
+
+    def prepare(j):
+        for copy in pass_copies[j]:
+            copy.wait_recv()
+        cols = slice(j * width, (j + 1) * width)
+        for s in range(outer_size):
+            rows = slice(s * months_local, (s + 1) * months_local)
+            nf_ref[rows, cols] = nf_all[s, :, cols] * fee_row[:, cols]
+            mf_ref[rows, cols] = mort_all[s, :, cols] * death[:, cols]
+            om_ref[rows, cols] = 1.0 - mort_all[s, :, cols]
 
     def start_one(cols):
         scale = fee[0:1, cols]
@@ -350,19 +349,31 @@
     def start_two(cols):
         return state_one[0, :, cols], state_one[1, :, cols], state_one[2, :, cols]
 
-    year(start_one, plans, cell, gw, 0, state_one, width)
     split = -(-outers // 2)
     halves = [(low, high) for low, high in ((0, split), (split, outers)) if low < high]
     distances = len(group_others)
     one_copies = []
     for h, (low, high) in enumerate(halves):
-        inner(state_one, plans, cell, gb, db_one, PERIOD, low, high, paths, sums, width)
+        if h == 0:
+            for j in range(chunks):
+                prepare(j)
+                year(start_one, plans, cell, gw, 0, state_one, width, j, j + 1)
+                inner(state_one, plans, cell, gb, db_one, PERIOD, low, high, paths, sums, width, j, j + 1)
+                if j == 0:
+                    for later in range(ahead, chunks):
+                        pass_on(later)
+                    relay(2, rounds)
+        else:
+            inner(state_one, plans, cell, gb, db_one, PERIOD, low, high, paths, sums, width, 0, chunks)
         reduce_rows(sums, first, low, high, 1.0 / paths_all)
         slots_one[h, group] = local_totals(first, low, high)
         if h == 0:
-            for part in plan_copies:
-                for piece in part:
+            for copies in plan_copies:
+                for piece in copies:
                     piece[4].wait_send()
+            for copies in pass_copies:
+                for copy in copies:
+                    copy.wait_send()
             pl.semaphore_wait(relay_sems.at[rounds - 1], near)
         slot = slots_one.at[h, group]
         one_copies.append(
@@ -390,9 +401,9 @@
         total_one = total_one + jnp.sum(slots_one[h], axis=0)
         spread_two = (spread_one * (1.0 + jnp.tanh(total_one / cells_all)))[:, 0:1]
         spread_lanes(1.0 + jnp.maximum(world_rows[:, PERIOD:] - spread_two, credit_floor), gw, everything)
-        year(start_two, plans, cell, gw, PERIOD, state_two, width)
+        year(start_two, plans, cell, gw, PERIOD, state_two, width, 0, chunks)
         fill_growth(second_rates, spread_two, gb, low, high, paths)
-        inner(state_two, plans, cell, gb, db_two, 2 * PERIOD, low, high, paths, sums, width)
+        inner(state_two, plans, cell, gb, db_two, 2 * PERIOD, low, high, paths, sums, width, 0, chunks)
         reduce_rows(sums, second, low, high, 1.0 / paths_all)
     discount = jnp.exp(-jnp.sum(world_rows[:, PERIOD:], axis=1, keepdims=True))
     mine_one = slots_one[0, group]
@@ -519,7 +530,7 @@
     def sems(count):
         return pltpu.SemaphoreType.DMA((2, max(count, 1)))
 
-    chunks = months_local // ROWS if months_local % ROWS == 0 else 1
+    chunks = cells_local // width
     plan_count = 2 * chunks * (outer_size - 1)
     plan = buffer(months, cells_local)
     gathered = buffer(outer_size, months_local, cells_local)

time: 41.2 us -> 39.1 us (0.949)
  Pallas kernels: 40.4 us -> 38.3 us
    pallas_call x1, Pallas kernels: 39.8 us -> 37.7 us  [body(): pl.pallas_call(functools.partial(whole_kernel, outers, paths, paths_all,...]
where the time goes in v4:
time: 39.1 us; the launch traced here: 39 us
  Pallas kernels  38.3 us (98%)
  between operations  0.64 us (2%)
    pallas_call x1, Pallas kernels, body(): pl.pallas_call(functools.partial(whole_kernel, outers, paths, paths_all,...  37.7 us

profile of v4, /device:TPU:0, one launch (start us, length us, event | category | flops | bytes accessed | tf_op | source)
XLA Modules:
  0.0 39.0 jit_solution(3336944574497697992)
XLA Ops:
  0.6 37.7 %shard_map.157 = (f32[2,1,1,2048]{3,2,1,0:T(1,128)S(1)}, f32[2,1,1,64]{3,2,1,0:T(1,128)S(1)}, f32[1,128]{1,0:T(1,128)S(1)}) custom-call(f32[24,2048]{1,0:T(8,128)} %premium.1, f32[24,2048]{1,0:T(8,128)} %charge.1, f32[24,2048]{1,0:T(8,128)} %mortality.1, f32[16,48]{1,0:T(8,128)} %table_in.1, s32[1,2048]{1,0:T(1,128)} %bitcast.16, s32[1,2048]{1,0:T(1,128)} %bitcast.17, ...), custom_call_target="tpu_custom_call" | custom-call | tf_op jit(solution)/shard_map/pallas_call | solution.py:545
  38.3 0.6 %shard_map.158 = (f32[2,1,1,2048]{3,2,1,0:T(1,128)}, f32[2,1,1,64]{3,2,1,0:T(1,128)}, f32[1,1]{1,0:T(1,128)}) custom-call(f32[2,1,1,2048]{3,2,1,0:T(1,128)S(1)} %get-tuple-element.9.reserve, f32[2,1,1,64]{3,2,1,0:T(1,128)S(1)} %get-tuple-element.10.block, f32[1,128]{1,0:T(1,128)S(1)} %get-tuple-element.11.capital), custom_call_target="tpu_custom_call" | custom-call | tf_op jit(solution)/shard_map/pallas_call | solution.py:574

commit v5 on v4

--- a/solution.py
+++ b/solution.py
@@ -82,12 +82,14 @@
     lax.fori_loop(begin, end, chunk, 0)
 
 
-def inner(state, plans, cell, gb, db, first_month, low, high, paths, sums, width, begin, end):
+def inner(state, plans, cell, gb, db, first_month, low, high, paths, sums, width, begin, end, flows):
     nf_ref, mf_ref, om_ref, lb_ref = plans
     repeat = width // LANES
     months = db.shape[0]
     groups = paths // ROWS
     chunks = end - begin
+    base = first_month // ROWS * ROWS
+    top = -(-(first_month + PERIOD) // ROWS) * ROWS
 
     def block(step, _):
         o, j = low + step // chunks, begin + step % chunks
@@ -95,26 +97,36 @@
         keep, ratchet, rollup = cell[0:1, cols], cell[1:2, cols], cell[2:3, cols]
         shape = (ROWS, width)
         one = pl.ds(o, 1)
-        account = [jnp.broadcast_to(state[0, one, cols], shape)] * groups
-        surviving = [jnp.broadcast_to(state[1, one, cols], shape)] * groups
-        guarantee = [jnp.broadcast_to(state[2, one, cols], shape)] * groups
-        inverse = [1.0 / guarantee[0]] * groups
+        guarantee = state[2, one, cols]
+        across = 1.0 / guarantee
+        flows[: top - base, :] = nf_ref[base:top, cols] * across
+        ratio = [jnp.broadcast_to(state[0, one, cols] * across, shape)] * groups
+        weight = [jnp.broadcast_to(state[1, one, cols] * guarantee, shape)] * groups
+        inverse = [jnp.broadcast_to(across, shape)] * groups
         rows = [pl.ds(pl.multiple_of(o * paths + g * ROWS, ROWS), ROWS) for g in range(groups)]
         present = jnp.zeros(shape, jnp.float32)
         for m in range(months):
             row = slice(first_month + m, first_month + m + 1)
-            nf, mf, om, lb = nf_ref[row, cols], mf_ref[row, cols], om_ref[row, cols], lb_ref[row, cols]
+            mf, om, lb = mf_ref[row, cols], om_ref[row, cols], lb_ref[row, cols]
             for g in range(groups):
-                before, alive = account[g], surviving[g]
-                account[g], surviving[g] = month(
-                    before, alive, tiles(gb[m, rows[g], :], repeat), nf, om, lb, keep, inverse[g]
-                )
-                claims = claims_of(before, account[g], alive, guarantee[g], mf)
+                if m < PERIOD:
+                    at = first_month - base + m
+                    nf = flows[at : at + 1, :]
+                else:
+                    nf = nf_ref[row, cols] * inverse[g]
+                before, alive = ratio[g], weight[g]
+                after = jnp.maximum(before * keep + nf, 0.0) * tiles(gb[m, rows[g], :], repeat)
+                weight[g] = alive * (om - lb * jnp.clip(after, 0.5, 1.5))
+                claims = alive * (mf * jnp.maximum(1.0 - after, 0.0) - before)
                 present = present + tiles(db[m, rows[g], :], repeat) * claims
+                ratio[g] = after
             if (m + 1) % PERIOD == 0 and m + 1 < months:
                 for g in range(groups):
-                    guarantee[g] = anniversary(account[g], guarantee[g], ratchet, rollup)
-                    inverse[g] = 1.0 / guarantee[g]
+                    lift = 1.0 + ratchet * (jnp.maximum(ratio[g], 1.0) - 1.0) + rollup * rollup_growth
+                    drop = 1.0 / lift
+                    ratio[g] = ratio[g] * drop
+                    weight[g] = weight[g] * lift
+                    inverse[g] = inverse[g] * drop
         sums[o, :, cols] = present
         return 0
 
@@ -133,6 +145,14 @@
             spread_lanes(
                 1.0 + jnp.maximum(rates_ref[rows, :] - spread_column[o : o + 1], credit_floor), gb, rows
             )
+
+
+def fill_later_growth(rates_lanes, spread_column, gb, low, high, paths):
+    for o in range(low, high):
+        rows = slice(o * paths, (o + 1) * paths)
+        less = jnp.broadcast_to(spread_column[o : o + 1], (paths, LANES))
+        for m in range(rates_lanes.shape[0]):
+            gb[m, rows, :] = 1.0 + jnp.maximum(rates_lanes[m, rows, :] - less, credit_floor)
 
 
 def fill_discount(rates_ref, db):
@@ -223,7 +243,7 @@
     v_premium, v_charge, table, lapse, kind, block_row, account, guarantee, fee,
     first_rates, second_rates, world, spread,
     nf_all, mort_all, nf_ref, mf_ref, om_ref, lb_ref, cell, state_one, state_two,
-    gb, db_one, db_two, gw, sums, first, second,
+    gb, db_one, db_two, rb_two, flows, gw, sums, first, second,
     slots_one, slots_two, kept_slots, hot, term_slots, term_out, loss_slots,
     load_sems, plan_sems, pass_sems, one_sems, total_sems, kept_sems, term_sems, loss_sems, relay_sems,
 ):
@@ -317,6 +337,8 @@
     fill_growth(first_rates, spread_one, gb, 0, outers, paths)
     fill_discount(first_rates, db_one)
     fill_discount(second_rates, db_two)
+    for at in range(0, second_rates.shape[0], ROWS):
+        spread_lanes(second_rates[at : at + ROWS, :], rb_two, slice(at, at + ROWS))
     hot[...] = (
         lax.broadcasted_iota(jnp.int32, (blocks, cells_local), 0) == block_row[...]
     ).astype(jnp.float32).astype(jnp.bfloat16)
@@ -358,13 +380,13 @@
             for j in range(chunks):
                 prepare(j)
                 year(start_one, plans, cell, gw, 0, state_one, width, j, j + 1)
-                inner(state_one, plans, cell, gb, db_one, PERIOD, low, high, paths, sums, width, j, j + 1)
+                inner(state_one, plans, cell, gb, db_one, PERIOD, low, high, paths, sums, width, j, j + 1, flows)
                 if j == 0:
                     for later in range(ahead, chunks):
                         pass_on(later)
                     relay(2, rounds)
         else:
-            inner(state_one, plans, cell, gb, db_one, PERIOD, low, high, paths, sums, width, 0, chunks)
+            inner(state_one, plans, cell, gb, db_one, PERIOD, low, high, paths, sums, width, 0, chunks, flows)
         reduce_rows(sums, first, low, high, 1.0 / paths_all)
         slots_one[h, group] = local_totals(first, low, high)
         if h == 0:
@@ -402,8 +424,8 @@
         spread_two = (spread_one * (1.0 + jnp.tanh(total_one / cells_all)))[:, 0:1]
         spread_lanes(1.0 + jnp.maximum(world_rows[:, PERIOD:] - spread_two, credit_floor), gw, everything)
         year(start_two, plans, cell, gw, PERIOD, state_two, width, 0, chunks)
-        fill_growth(second_rates, spread_two, gb, low, high, paths)
-        inner(state_two, plans, cell, gb, db_two, 2 * PERIOD, low, high, paths, sums, width, 0, chunks)
+        fill_later_growth(rb_two, spread_two, gb, low, high, paths)
+        inner(state_two, plans, cell, gb, db_two, 2 * PERIOD, low, high, paths, sums, width, 0, chunks, flows)
         reduce_rows(sums, second, low, high, 1.0 / paths_all)
     discount = jnp.exp(-jnp.sum(world_rows[:, PERIOD:], axis=1, keepdims=True))
     mine_one = slots_one[0, group]
@@ -557,7 +579,8 @@
             gathered, gathered, plan, plan, plan, plan, buffer(ROWS, cells_local),
             buffer(3, ROWS, cells_local), buffer(3, ROWS, cells_local),
             buffer(first_months, total_rows, LANES), buffer(first_months, total_rows, LANES),
-            buffer(second_months, total_rows, LANES), buffer(PERIOD, ROWS, LANES),
+            buffer(second_months, total_rows, LANES), buffer(second_months, total_rows, LANES),
+            buffer(PERIOD + 2 * ROWS, width), buffer(PERIOD, ROWS, LANES),
             buffer(outers, ROWS, cells_local), buffer(outers, 1, cells_local), buffer(outers, 1, cells_local),
             buffer(2, group_size, ROWS, LANES), buffer(wide_count, 1, LANES),
             buffer(2, inner_size, kept, 1, cells_local), buffer(blocks, cells_local, dtype=jnp.bfloat16),

time: 39.1 us -> 38.4 us (0.982)
  Pallas kernels: 38.3 us -> 37.6 us
    pallas_call x1, Pallas kernels: 37.7 us -> 37 us  [body(): pl.pallas_call(functools.partial(whole_kernel, outers, paths, paths_all,...]
where the time goes in v5:
time: 38.4 us; the launch traced here: 38.3 us
  Pallas kernels  37.6 us (98%)
  between operations  0.64 us (2%)
    pallas_call x1, Pallas kernels, body(): pl.pallas_call(functools.partial(whole_kernel, outers, paths, paths_all,...  37 us

profile of v5, /device:TPU:0, one launch (start us, length us, event | category | flops | bytes accessed | tf_op | source)
XLA Modules:
  0.0 38.3 jit_solution(8132778321692533300)
XLA Ops:
  0.6 37.0 %shard_map.157 = (f32[2,1,1,2048]{3,2,1,0:T(1,128)S(1)}, f32[2,1,1,64]{3,2,1,0:T(1,128)S(1)}, f32[1,128]{1,0:T(1,128)S(1)}) custom-call(f32[24,2048]{1,0:T(8,128)} %premium.1, f32[24,2048]{1,0:T(8,128)} %charge.1, f32[24,2048]{1,0:T(8,128)} %mortality.1, f32[16,48]{1,0:T(8,128)} %table_in.1, s32[1,2048]{1,0:T(1,128)} %bitcast.16, s32[1,2048]{1,0:T(1,128)} %bitcast.17, ...), custom_call_target="tpu_custom_call" | custom-call | tf_op jit(solution)/shard_map/pallas_call | solution.py:567
  37.6 0.6 %shard_map.158 = (f32[2,1,1,2048]{3,2,1,0:T(1,128)}, f32[2,1,1,64]{3,2,1,0:T(1,128)}, f32[1,1]{1,0:T(1,128)}) custom-call(f32[2,1,1,2048]{3,2,1,0:T(1,128)S(1)} %get-tuple-element.9.reserve, f32[2,1,1,64]{3,2,1,0:T(1,128)S(1)} %get-tuple-element.10.block, f32[1,128]{1,0:T(1,128)S(1)} %get-tuple-element.11.capital), custom_call_target="tpu_custom_call" | custom-call | tf_op jit(solution)/shard_map/pallas_call | solution.py:597

commit v6 on v5

--- a/solution.py
+++ b/solution.py
@@ -99,7 +99,7 @@
         one = pl.ds(o, 1)
         guarantee = state[2, one, cols]
         across = 1.0 / guarantee
-        flows[: top - base, :] = nf_ref[base:top, cols] * across
+        flows[: top - base, :width] = nf_ref[base:top, cols] * across
         ratio = [jnp.broadcast_to(state[0, one, cols] * across, shape)] * groups
         weight = [jnp.broadcast_to(state[1, one, cols] * guarantee, shape)] * groups
         inverse = [jnp.broadcast_to(across, shape)] * groups
@@ -111,7 +111,7 @@
             for g in range(groups):
                 if m < PERIOD:
                     at = first_month - base + m
-                    nf = flows[at : at + 1, :]
+                    nf = flows[at : at + 1, :width]
                 else:
                     nf = nf_ref[row, cols] * inverse[g]
                 before, alive = ratio[g], weight[g]
@@ -161,6 +161,12 @@
         spread_lanes(discount[at : at + ROWS], db, slice(at, at + ROWS))
 
 
+def spans_of(total, width):
+    head = width // 2
+    spans = [(0, head), (head, head)] if head % (2 * LANES) == 0 else [(0, width)]
+    return spans + [(begin, width) for begin in range(width, total, width)]
+
+
 def peers(axes):
     sizes = [lax.axis_size(axis) for axis in axes]
     count = 1
@@ -243,7 +249,7 @@
     v_premium, v_charge, table, lapse, kind, block_row, account, guarantee, fee,
     first_rates, second_rates, world, spread,
     nf_all, mort_all, nf_ref, mf_ref, om_ref, lb_ref, cell, state_one, state_two,
-    gb, db_one, db_two, rb_two, flows, gw, sums, first, second,
+    gb, db_one, db_two, rb_two, flows, gw, world_lanes, spread_wide, sums, first, second,
     slots_one, slots_two, kept_slots, hot, term_slots, term_out, loss_slots,
     load_sems, plan_sems, pass_sems, one_sems, total_sems, kept_sems, term_sems, loss_sems, relay_sems,
 ):
@@ -280,11 +286,12 @@
 
     pair = inner_size % 2 == 0
     chunks = cells_local // width
-    part = width // 2 if pair else width
+    spans = spans_of(cells_local, width)
     side = lax.rem(inner_me, 2) if pair else 0
     plan_copies = []
-    for j in range(chunks):
-        mine = pl.ds(pl.multiple_of(j * width + side * part, part), part)
+    for j, (begin, size) in enumerate(spans):
+        part = size // 2 if pair else size
+        mine = pl.ds(pl.multiple_of(begin + side * part, part), part)
         copies = []
         for d, (_, device) in enumerate(outer_others):
             for k, plan in enumerate((nf_all, mort_all)):
@@ -334,6 +341,8 @@
     spread_one = jnp.sum(jnp.where(diagonal, spread[...], 0.0), axis=1, keepdims=True)
     everything = slice(0, ROWS)
     spread_lanes(1.0 + jnp.maximum(world_rows[:, :PERIOD] - spread_one, credit_floor), gw, everything)
+    spread_lanes(world_rows[:, PERIOD : 2 * PERIOD], world_lanes, everything)
+    spread_wide[...] = jnp.broadcast_to(spread_one, spread_wide.shape)
     fill_growth(first_rates, spread_one, gb, 0, outers, paths)
     fill_discount(first_rates, db_one)
     fill_discount(second_rates, db_two)
@@ -342,7 +351,7 @@
     hot[...] = (
         lax.broadcasted_iota(jnp.int32, (blocks, cells_local), 0) == block_row[...]
     ).astype(jnp.float32).astype(jnp.bfloat16)
-    ahead = min(2, chunks)
+    ahead = min(2, len(spans))
     for j in range(ahead):
         pass_on(j)
     relay(1, 2)
@@ -352,7 +361,8 @@
     def prepare(j):
         for copy in pass_copies[j]:
             copy.wait_recv()
-        cols = slice(j * width, (j + 1) * width)
+        begin, size = spans[j]
+        cols = slice(begin, begin + size)
         for s in range(outer_size):
             rows = slice(s * months_local, (s + 1) * months_local)
             nf_ref[rows, cols] = nf_all[s, :, cols] * fee_row[:, cols]
@@ -361,7 +371,7 @@
 
     def start_one(cols):
         scale = fee[0:1, cols]
-        shape = (ROWS, width)
+        shape = (ROWS, cols.size)
         return (
             jnp.broadcast_to(account[0:1, cols] * scale, shape),
             jnp.ones(shape, jnp.float32),
@@ -377,13 +387,16 @@
     one_copies = []
     for h, (low, high) in enumerate(halves):
         if h == 0:
-            for j in range(chunks):
+            for j, (begin, size) in enumerate(spans):
                 prepare(j)
-                year(start_one, plans, cell, gw, 0, state_one, width, j, j + 1)
-                inner(state_one, plans, cell, gb, db_one, PERIOD, low, high, paths, sums, width, j, j + 1, flows)
+                at = begin // size
+                year(start_one, plans, cell, gw, 0, state_one, size, at, at + 1)
+                inner(
+                    state_one, plans, cell, gb, db_one, PERIOD, low, high, paths, sums, size, at, at + 1, flows
+                )
+                if j + ahead < len(spans):
+                    pass_on(j + ahead)
                 if j == 0:
-                    for later in range(ahead, chunks):
-                        pass_on(later)
                     relay(2, rounds)
         else:
             inner(state_one, plans, cell, gb, db_one, PERIOD, low, high, paths, sums, width, 0, chunks, flows)
@@ -421,8 +434,9 @@
     for h, (low, high) in enumerate(halves):
         finish(one_copies[h])
         total_one = total_one + jnp.sum(slots_one[h], axis=0)
-        spread_two = (spread_one * (1.0 + jnp.tanh(total_one / cells_all)))[:, 0:1]
-        spread_lanes(1.0 + jnp.maximum(world_rows[:, PERIOD:] - spread_two, credit_floor), gw, everything)
+        spread_two = spread_wide[...] * (1.0 + jnp.tanh(total_one / cells_all))
+        for m in range(PERIOD):
+            gw[m] = 1.0 + jnp.maximum(world_lanes[m] - spread_two, credit_floor)
         year(start_two, plans, cell, gw, PERIOD, state_two, width, 0, chunks)
         fill_later_growth(rb_two, spread_two, gb, low, high, paths)
         inner(state_two, plans, cell, gb, db_two, 2 * PERIOD, low, high, paths, sums, width, 0, chunks, flows)
@@ -552,7 +566,7 @@
     def sems(count):
         return pltpu.SemaphoreType.DMA((2, max(count, 1)))
 
-    chunks = cells_local // width
+    chunks = len(spans_of(cells_local, width))
     plan_count = 2 * chunks * (outer_size - 1)
     plan = buffer(months, cells_local)
     gathered = buffer(outer_size, months_local, cells_local)
@@ -581,6 +595,7 @@
             buffer(first_months, total_rows, LANES), buffer(first_months, total_rows, LANES),
             buffer(second_months, total_rows, LANES), buffer(second_months, total_rows, LANES),
             buffer(PERIOD + 2 * ROWS, width), buffer(PERIOD, ROWS, LANES),
+            buffer(PERIOD, ROWS, LANES), buffer(ROWS, LANES),
             buffer(outers, ROWS, cells_local), buffer(outers, 1, cells_local), buffer(outers, 1, cells_local),
             buffer(2, group_size, ROWS, LANES), buffer(wide_count, 1, LANES),
             buffer(2, inner_size, kept, 1, cells_local), buffer(blocks, cells_local, dtype=jnp.bfloat16),

time: 38.4 us -> 37.9 us (0.987)
  Pallas kernels: 37.6 us -> 37.1 us
    pallas_call x1, Pallas kernels: 37 us -> 36.5 us  [body(): pl.pallas_call(functools.partial(whole_kernel, outers, paths, paths_all,...]
where the time goes in v6:
time: 37.9 us; the launch traced here: 37.7 us
  Pallas kernels  37.1 us (98%)
  between operations  0.64 us (2%)
    pallas_call x1, Pallas kernels, body(): pl.pallas_call(functools.partial(whole_kernel, outers, paths, paths_all,...  36.5 us

profile of v6, /device:TPU:0, one launch (start us, length us, event | category | flops | bytes accessed | tf_op | source)
XLA Modules:
  0.0 37.7 jit_solution(16352937521404218929)
XLA Ops:
  0.6 36.5 %shard_map.157 = (f32[2,1,1,2048]{3,2,1,0:T(1,128)S(1)}, f32[2,1,1,64]{3,2,1,0:T(1,128)S(1)}, f32[1,128]{1,0:T(1,128)S(1)}) custom-call(f32[24,2048]{1,0:T(8,128)} %premium.1, f32[24,2048]{1,0:T(8,128)} %charge.1, f32[24,2048]{1,0:T(8,128)} %mortality.1, f32[16,48]{1,0:T(8,128)} %table_in.1, s32[1,2048]{1,0:T(1,128)} %bitcast.16, s32[1,2048]{1,0:T(1,128)} %bitcast.17, ...), custom_call_target="tpu_custom_call" | custom-call | tf_op jit(solution)/shard_map/pallas_call | solution.py:581
  37.1 0.6 %shard_map.158 = (f32[2,1,1,2048]{3,2,1,0:T(1,128)}, f32[2,1,1,64]{3,2,1,0:T(1,128)}, f32[1,1]{1,0:T(1,128)}) custom-call(f32[2,1,1,2048]{3,2,1,0:T(1,128)S(1)} %get-tuple-element.9.reserve, f32[2,1,1,64]{3,2,1,0:T(1,128)S(1)} %get-tuple-element.10.block, f32[1,128]{1,0:T(1,128)S(1)} %get-tuple-element.11.capital), custom_call_target="tpu_custom_call" | custom-call | tf_op jit(solution)/shard_map/pallas_call | solution.py:612

commit v7 on v6

--- a/solution.py
+++ b/solution.py
@@ -348,12 +348,13 @@
     fill_discount(second_rates, db_two)
     for at in range(0, second_rates.shape[0], ROWS):
         spread_lanes(second_rates[at : at + ROWS, :], rb_two, slice(at, at + ROWS))
-    hot[...] = (
-        lax.broadcasted_iota(jnp.int32, (blocks, cells_local), 0) == block_row[...]
-    ).astype(jnp.float32).astype(jnp.bfloat16)
     ahead = min(2, len(spans))
     for j in range(ahead):
         pass_on(j)
+        if j == 0:
+            hot[...] = (
+                lax.broadcasted_iota(jnp.int32, (blocks, cells_local), 0) == block_row[...]
+            ).astype(jnp.float32).astype(jnp.bfloat16)
     relay(1, 2)
     death = 1.0 / fee_row
     plans = (nf_ref, mf_ref, om_ref, lb_ref)
@@ -453,7 +454,7 @@
     slots_two[place] = jnp.sum(mine_loss, axis=0, keepdims=True)
     total_copies = [
         send(slots_two.at[place], slots_two.at[place], device, total_sems, d)
-        for d, (_, device) in enumerate(others)
+        for d, (_, device) in enumerate(others[::-1])
     ]
     send_kept(1, second)
     step = -(-outers // ROWS) * ROWS

time: 37.9 us -> 37.8 us (level)
  no operation moved by 1% of the time
where the time goes in v7:
time: 37.8 us; the launch traced here: 37.7 us
  Pallas kernels  37 us (98%)
  between operations  0.64 us (2%)
    pallas_call x1, Pallas kernels, body(): pl.pallas_call(functools.partial(whole_kernel, outers, paths, paths_all,...  36.4 us

profile of v7, /device:TPU:0, one launch (start us, length us, event | category | flops | bytes accessed | tf_op | source)
XLA Modules:
  0.0 37.7 jit_solution(1449473105500126403)
XLA Ops:
  0.6 36.4 %shard_map.157 = (f32[2,1,1,2048]{3,2,1,0:T(1,128)S(1)}, f32[2,1,1,64]{3,2,1,0:T(1,128)S(1)}, f32[1,128]{1,0:T(1,128)S(1)}) custom-call(f32[24,2048]{1,0:T(8,128)} %premium.1, f32[24,2048]{1,0:T(8,128)} %charge.1, f32[24,2048]{1,0:T(8,128)} %mortality.1, f32[16,48]{1,0:T(8,128)} %table_in.1, s32[1,2048]{1,0:T(1,128)} %bitcast.16, s32[1,2048]{1,0:T(1,128)} %bitcast.17, ...), custom_call_target="tpu_custom_call" | custom-call | tf_op jit(solution)/shard_map/pallas_call | solution.py:582
  37.0 0.6 %shard_map.158 = (f32[2,1,1,2048]{3,2,1,0:T(1,128)}, f32[2,1,1,64]{3,2,1,0:T(1,128)}, f32[1,1]{1,0:T(1,128)}) custom-call(f32[2,1,1,2048]{3,2,1,0:T(1,128)S(1)} %get-tuple-element.9.reserve, f32[2,1,1,64]{3,2,1,0:T(1,128)S(1)} %get-tuple-element.10.block, f32[1,128]{1,0:T(1,128)S(1)} %get-tuple-element.11.capital), custom_call_target="tpu_custom_call" | custom-call | tf_op jit(solution)/shard_map/pallas_call | solution.py:613
